TPU v7x, 128 devices: a whole 4x4x4 slice. The times are simulated.
128 devices in a mesh: gx: 16 (over y, x), gy: 8 (over z, core).
Axes of the slice: x: 4, y: 4, z: 4, core: 2. Of those that a mesh axis runs over, the one named last changes fastest.
Arguments:
- objects: float32 [4, 8192, 4096], P(None, 'gx', 'gy'), may hold values from -3 to 3
- probe_wave: float32 [2, 256, 256], replicated, may hold values from -5 to 5
- prop_phase: float32 [256, 256], replicated, may hold values from -3.140625 to 3.140625
- intensity: float32 [512, 256, 256], P(('gx', 'gy')), may hold values from 0 to 1
- offsets: int32 [512, 2], P(('gx', 'gy')), may hold values from 0 to 512
- counts: int32 [128], P(('gx', 'gy')), may hold values from 1 to 4, 256 in all
Outputs:
- gradient: float32 [4, 8192, 4096], P(None, 'gx', 'gy')
Inputs may be any that keep to these rules, and one draw needn't show every extreme that they name: `counts`: every device has at least one live frame; the busiest has exactly 4.
All inputs are finite; a program needn't handle non-finite values.
Results may differ from a plain program's by a relative error of at most 0.00014.
Values sent between devices are 32-bit elements; how exact they have to be, the bound alone decides.
A program may use at most 128 MiB of HBM per device.

v0:
```python
import math

import jax
import jax.numpy as jnp
from jax import lax
from jax.sharding import PartitionSpec as P

HIGH = lax.Precision.HIGHEST


def with_halo(cells, sides, width):
    for axis, dim in sides:
        count = lax.axis_size(axis)
        ends = count - 1
        head = lax.slice_in_dim(cells, 0, width, axis=dim)
        tail = lax.slice_in_dim(cells, cells.shape[dim] - width, cells.shape[dim], axis=dim)
        cells = jnp.concatenate(
            [
                lax.ppermute(tail, axis, [(i, (i + 1) % count) for i in range(ends)]),
                cells,
                lax.ppermute(head, axis, [((i + 1) % count, i) for i in range(ends)]),
            ],
            axis=dim,
        )
    return cells


def shifted(block, axis, distance):
    devices = range(lax.axis_size(axis))
    route = [(i - distance, i) for i in devices if i - distance in devices]
    return lax.ppermute(block, axis, route)


def product(left, right):
    return jnp.dot(left, right, precision=HIGH, preferred_element_type=jnp.float32)


def complex_product(left_re, left_im, right_re, right_im):
    return (
        product(left_re, right_re) - product(left_im, right_im),
        product(left_re, right_im) + product(left_im, right_re),
    )


def transform(real_part, imag_part, cosine, sine_part):
    upper_re, upper_im = complex_product(cosine, sine_part, real_part, imag_part)
    return complex_product(upper_re, upper_im, cosine, sine_part)


def times(left_re, left_im, right_re, right_im):
    return (left_re * right_re - left_im * right_im, left_re * right_im + left_im * right_re)


def conj_times(left_re, left_im, right_re, right_im):
    return (left_re * right_re + left_im * right_im, left_re * right_im - left_im * right_re)


def tables(frame_len, probe_wave, prop_phase):
    indices = jnp.arange(frame_len, dtype=jnp.int32)
    wrapped = indices[:, None] * indices[None, :] % frame_len
    angles = wrapped.astype(jnp.float32) * (2.0 * math.pi / frame_len)
    factor = 1.0 / math.sqrt(frame_len)
    cosine = jnp.cos(angles) * factor
    sine_part = jnp.sin(angles) * factor
    return (
        cosine,
        -sine_part,
        sine_part,
        probe_wave[0],
        probe_wave[1],
        jnp.cos(prop_phase),
        jnp.sin(prop_phase),
    )


def frame_gradient(window, measured, constants):
    cosine, forward_sine, inverse_sine, probe_re, probe_im, wave_re, wave_im = constants
    enter_re, enter_im = times(probe_re, probe_im, window[0], window[1])
    spec_re, spec_im = transform(enter_re, enter_im, cosine, forward_sine)
    spec_re, spec_im = times(wave_re, wave_im, spec_re, spec_im)
    carry_re, carry_im = transform(spec_re, spec_im, cosine, inverse_sine)
    exit_re, exit_im = times(carry_re, carry_im, window[2], window[3])
    far_re, far_im = transform(exit_re, exit_im, cosine, forward_sine)
    misfit = far_re * far_re + far_im * far_im - measured
    gexit_re, gexit_im = transform(misfit * far_re, misfit * far_im, cosine, inverse_sine)
    gtwo_re, gtwo_im = conj_times(carry_re, carry_im, gexit_re, gexit_im)
    gcarry_re, gcarry_im = conj_times(window[2], window[3], gexit_re, gexit_im)
    back_re, back_im = transform(gcarry_re, gcarry_im, cosine, forward_sine)
    back_re, back_im = conj_times(wave_re, wave_im, back_re, back_im)
    genter_re, genter_im = transform(back_re, back_im, cosine, inverse_sine)
    gone_re, gone_im = conj_times(probe_re, probe_im, genter_re, genter_im)
    return jnp.stack([gone_re, gone_im, gtwo_re, gtwo_im])


def shards(objects, probe_wave, prop_phase, intensity, offsets, counts):
    frame_len = intensity.shape[1]
    margin = frame_len // 2
    constants = tables(frame_len, probe_wave, prop_phase)
    padded = with_halo(objects, (("gx", 1), ("gy", 2)), margin)
    summed = jnp.zeros(padded.shape, jnp.float32)
    own_count = counts[0]
    anchor = jnp.int32(0)

    def window_at(source, row_start, col_start):
        return lax.dynamic_slice(source, (anchor, row_start, col_start), (4, frame_len, frame_len))

    def add_window(running, update, row_start, col_start):
        current = window_at(running, row_start, col_start)
        return lax.dynamic_update_slice(running, current + update, (anchor, row_start, col_start))

    def own_step(frame_slot, running):
        row_start = offsets[frame_slot, 0]
        col_start = offsets[frame_slot, 1]
        measured = lax.dynamic_index_in_dim(intensity, frame_slot, 0, keepdims=False)
        update = frame_gradient(window_at(padded, row_start, col_start), measured, constants)
        return add_window(running, update, row_start, col_start)

    summed = lax.fori_loop(0, own_count, own_step, summed)
    from_below = shifted(summed[:, :margin, :], "gx", -1)
    from_above = shifted(summed[:, -margin:, :], "gx", 1)
    inner = summed[:, margin:-margin, :]
    inner = inner.at[:, :margin, :].add(from_above).at[:, -margin:, :].add(from_below)
    from_right = shifted(inner[:, :, :margin], "gy", -1)
    from_left = shifted(inner[:, :, -margin:], "gy", 1)
    folded = inner[:, :, margin:-margin]
    folded = folded.at[:, :, :margin].add(from_left).at[:, :, -margin:].add(from_right)
    return folded


def solution(mesh):
    return jax.shard_map(
        shards,
        mesh=mesh,
        in_specs=(
            P(None, "gx", "gy"),
            P(),
            P(),
            P(("gx", "gy"), None, None),
            P(("gx", "gy"), None),
            P(("gx", "gy")),
        ),
        out_specs=P(None, "gx", "gy"),
        check_vma=False,
    )
```

profile of v0, /device:TPU:79, one launch (start us, length us, event | category | flops | bytes accessed | tf_op | source)
XLA Modules:
  0.0 567.4 jit_solution(1931269636991721500)
XLA Ops:
  0.0 1.9 fusion.297
  1.9 3.1 collective-permute-start
  5.1 2.2 collective-permute-start.1
  7.2 20.6 %collective-permute-done = f32[4,128,512]{2,1,0:T(8,128)S(1)} collective-permute-done((f32[4,128,512]{2,1,0:T(8,128)S(1)}, f32[4,128,512]{2,1,0:T(8,128)S(1)}, u32[]{:S(2)}, u32[]{:S(2)}) %collective-permute-start) | collective-permute-done | bytes 1048608 | tf_op jit(solution)/shard_map/ppermute | solution.py:19
  28.4 4.4 collective-permute-done.1
  32.9 2.6 copy-done
  35.5 1.9 fusion.296
  37.4 5.0 collective-permute-start.2
  42.4 1.9 collective-permute-start.3
  45.4 14.7 %collective-permute-done.2 = f32[4,768,128]{2,1,0:T(8,128)S(1)} collective-permute-done((f32[4,768,128]{2,1,0:T(8,128)}, f32[4,768,128]{2,1,0:T(8,128)S(1)}, u32[]{:S(2)}, u32[]{:S(2)}) %collective-permute-start.2) | collective-permute-done | bytes 1572896 | tf_op jit(solution)/shard_map/ppermute | solution.py:19
  60.1 4.4 collective-permute-done.3
  64.5 7.7 %pad_maximum_fusion = f32[4,768,768]{2,1,0:T(8,128)} fusion(f32[4,768,128]{2,1,0:T(8,128)} %collective-permute-done.3, f32[4,768,512]{2,1,0:T(8,128)} %copy-done, f32[4,768,128]{2,1,0:T(8,128)S(1)} %collective-permute-done.2), kind=kLoop, calls=%fused_computation.327 | loop fusion | flops 4718592 | bytes 18874368 | tf_op jit(solution)/shard_map/concatenate | solution.py:17
  72.2 4.4 broadcast_in_dim.2
  76.6 197.8 %while.16 = (s32[]{:T(128)}, f32[4,768,768]{2,1,0:T(8,128)}, s32[]{:T(128)}, s32[4,2]{0,1:T(2,128)S(1)}, f32[4,768,768]{2,1,0:T(8,128)}, /*index=5*/f32[256,256]...) while((s32[]{:T(128)}, f32[4,768,768]{2,1,0:T(8,128)}, ...), condition=%wide.region_1.2_spmd.clone.clone, body=%wide.region_0.1_spmd.clone.clone.sunk | while | flops 9717415936 | bytes 45613436 | solution.py:118
  91.0 1.5 fusion.489
  94.0 2.1 multiply_add_fusion.9
  97.6 1.5 convolution_subtract_fusion.21
  100.6 1.5 convolution_add_fusion.24
  102.1 1.5 fusion.495
  105.0 1.5 convolution_subtract_fusion.22
  106.5 2.8 multiply_add_fusion.10
  110.8 1.5 convolution_subtract_fusion.23
  113.8 1.5 convolution_add_fusion.25
  115.3 1.5 fusion.499
  118.3 1.5 convolution_subtract_fusion.24
  119.7 2.7 fusion.500
  123.9 1.5 convolution_subtract_fusion.25
  126.9 1.5 convolution_add_fusion.26
  132.8 3.1 multiply_subtract_fusion.7
  146.2 1.7 multiply_subtract_fusion.8
  158.2 1.5 add_bitcast_fusion.3
  159.7 1.8 maximum_add_fusion.2
  161.6 11.6 %dynamic_update_slice.6 = f32[4,768,768]{2,1,0:T(8,128)} dynamic-update-slice(f32[4,768,768]{2,1,0:T(8,128)} %get-tuple-element.532, f32[4,256,256]{2,1,0:T(8,128)S(1)} %maximum_add_fusion.2, s32[]{:T(128)} %constant.132.clone.1..sunk, s32[]{:T(128)S(6)} %select_n.307, s32[]{:T(128)S(6)} %select_n.308) | dynamic-update-slice | bytes 2097156 | tf_op jit(solution)/shard_map/while/body/dynamic_update_slice | solution.py:109
  187.6 1.5 fusion.489
  190.6 1.7 multiply_add_fusion.9
  193.8 1.5 convolution_subtract_fusion.21
  196.7 1.5 convolution_add_fusion.24
  198.2 1.5 fusion.495
  201.2 1.5 convolution_subtract_fusion.22
  202.7 2.9 multiply_add_fusion.10
  207.0 1.5 convolution_subtract_fusion.23
  210.0 1.5 convolution_add_fusion.25
  211.5 1.5 fusion.499
  214.4 1.5 convolution_subtract_fusion.24
  215.9 2.8 fusion.500
  220.3 1.5 convolution_subtract_fusion.25
  223.2 1.5 convolution_add_fusion.26
  229.1 2.9 multiply_subtract_fusion.7
  242.3 1.9 multiply_subtract_fusion.8
  254.6 1.5 add_bitcast_fusion.3
  256.1 1.8 maximum_add_fusion.2
  257.9 12.3 %dynamic_update_slice.6 = f32[4,768,768]{2,1,0:T(8,128)} dynamic-update-slice(f32[4,768,768]{2,1,0:T(8,128)} %get-tuple-element.532, f32[4,256,256]{2,1,0:T(8,128)S(1)} %maximum_add_fusion.2, s32[]{:T(128)} %constant.132.clone.1..sunk, s32[]{:T(128)S(6)} %select_n.307, s32[]{:T(128)S(6)} %select_n.308) | dynamic-update-slice | bytes 2097156 | tf_op jit(solution)/shard_map/while/body/dynamic_update_slice | solution.py:109
  274.5 1.5 slice.156
  276.0 194.0 %collective-permute-start.4 = (f32[4,128,768]{2,1,0:T(8,128)S(1)}, f32[4,128,768]{2,1,0:T(8,128)S(1)}, u32[]{:S(2)}, u32[]{:S(2)}) collective-permute-start(f32[4,128,768]{2,1,0:T(8,128)S(1)} %slice.156), channel_id=1, source_target_pairs={{0,8},{8,16},{16,24},{24,32},{32,40},{40,48},{48,56},{56,64},{64,7... | collective-permute-start | bytes 4718600 | tf_op jit(solution)/shard_map/ppermute | solution.py:31
  470.1 3.3 slice.154
  473.4 29.9 %collective-permute-done.4 = f32[4,128,768]{2,1,0:T(8,128)S(1)} collective-permute-done((f32[4,128,768]{2,1,0:T(8,128)S(1)}, f32[4,128,768]{2,1,0:T(8,128)S(1)}, u32[]{:S(2)}, u32[]{:S(2)}) %collective-permute-start.4) | collective-permute-done | bytes 1572896 | tf_op jit(solution)/shard_map/ppermute | solution.py:31
  503.3 2.3 fusion.294
  505.6 1.9 collective-permute-start.5
  507.5 38.7 %collective-permute-done.5 = f32[4,128,768]{2,1,0:T(8,128)S(1)} collective-permute-done((f32[4,128,768]{2,1,0:T(8,128)S(1)}, f32[4,128,768]{2,1,0:T(8,128)S(1)}, u32[]{:S(2)}, u32[]{:S(2)}) %collective-permute-start.5) | collective-permute-done | bytes 1572896 | tf_op jit(solution)/shard_map/ppermute | solution.py:31
  546.8 1.9 collective-permute-start.6
  548.7 2.4 collective-permute-start.7
  551.6 8.8 %collective-permute-done.6 = f32[4,512,128]{2,1,0:T(8,128)S(1)} collective-permute-done((f32[4,512,128]{2,1,0:T(8,128)S(1)}, f32[4,512,128]{2,1,0:T(8,128)S(1)}, u32[]{:S(2)}, u32[]{:S(2)}) %collective-permute-start.6) | collective-permute-done | bytes 1048608 | tf_op jit(solution)/shard_map/ppermute | solution.py:31
  560.6 4.2 collective-permute-done.7
  564.8 2.3 fusion.292
  (86 shorter events, 97.9 us)
Async XLA Ops:
  0.0 27.9 %copy-start.1 = (f32[4,512,512]{2,1,0:T(8,128)S(1)}, f32[4,512,512]{2,1,0:T(8,128)}, u32[]{:S(2)}) copy-start(f32[4,512,512]{2,1,0:T(8,128)} %param.16) | copy-start | bytes 12582916
  1.9 25.9 %collective-permute-start = (f32[4,128,512]{2,1,0:T(8,128)S(1)}, f32[4,128,512]{2,1,0:T(8,128)S(1)}, u32[]{:S(2)}, u32[]{:S(2)}) collective-permute-start(f32[4,128,512]{2,1,0:T(8,128)S(1)} %get-tuple-element.409), channel_id=1, source_target_pairs={{0,8},{8,16},{16,24},{24,32},{32,40},{40,48},{48,56},{56,64},{64,7... | collective-permute-start | bytes 3145736 | tf_op jit(solution)/shard_map/ppermute | solution.py:19
  5.1 27.7 %collective-permute-start.1 = (f32[4,128,512]{2,1,0:T(8,128)S(1)}, f32[4,128,512]{2,1,0:T(8,128)S(1)}, u32[]{:S(2)}, u32[]{:S(2)}) collective-permute-start(f32[4,128,512]{2,1,0:T(8,128)S(1)} %get-tuple-element.408), channel_id=1, source_target_pairs={{8,0},{16,8},{24,16},{32,24},{40,32},{48,40},{56,48},{64,56},{72,6... | collective-permute-start | bytes 3145736 | tf_op jit(solution)/shard_map/ppermute | solution.py:21
  28.4 16.0 %copy-start.3 = (f32[2,256,256]{2,1,0:T(8,128)S(1)}, f32[2,256,256]{2,1,0:T(8,128)}, u32[]{:S(2)}) copy-start(f32[2,256,256]{2,1,0:T(8,128)} %param.17) | copy-start | bytes 1572868
  28.4 16.0 %copy-start.4 = (f32[256,256]{1,0:T(8,128)S(1)}, f32[256,256]{1,0:T(8,128)}, u32[]{:S(2)}) copy-start(f32[256,256]{1,0:T(8,128)} %param.18) | copy-start | bytes 786436
  32.8 2.7 copy-start
  37.4 22.7 %collective-permute-start.2 = (f32[4,768,128]{2,1,0:T(8,128)}, f32[4,768,128]{2,1,0:T(8,128)S(1)}, u32[]{:S(2)}, u32[]{:S(2)}) collective-permute-start(f32[4,768,128]{2,1,0:T(8,128)} %get-tuple-element.406), channel_id=1, source_target_pairs={{0,1},{1,2},{2,3},{3,4},{4,5},{5,6},{6,7},{8,9},{9,10},{10,11},{11... | collective-permute-start | bytes 4718600 | tf_op jit(solution)/shard_map/ppermute | solution.py:19
  42.4 22.1 %collective-permute-start.3 = (f32[4,768,128]{2,1,0:T(8,128)}, f32[4,768,128]{2,1,0:T(8,128)}, u32[]{:S(2)}, u32[]{:S(2)}) collective-permute-start(f32[4,768,128]{2,1,0:T(8,128)} %get-tuple-element.407), channel_id=1, source_target_pairs={{1,0},{2,1},{3,2},{4,3},{5,4},{6,5},{7,6},{9,8},{10,9},{11,10},{12... | collective-permute-start | bytes 4718600 | tf_op jit(solution)/shard_map/ppermute | solution.py:21
  72.2 4.4 copy-start.5
  276.0 227.2 %collective-permute-start.4 = (f32[4,128,768]{2,1,0:T(8,128)S(1)}, f32[4,128,768]{2,1,0:T(8,128)S(1)}, u32[]{:S(2)}, u32[]{:S(2)}) collective-permute-start(f32[4,128,768]{2,1,0:T(8,128)S(1)} %slice.156), channel_id=1, source_target_pairs={{0,8},{8,16},{16,24},{24,32},{32,40},{40,48},{48,56},{56,64},{64,7... | collective-permute-start | bytes 4718600 | tf_op jit(solution)/shard_map/ppermute | solution.py:31
  505.6 40.7 %collective-permute-start.5 = (f32[4,128,768]{2,1,0:T(8,128)S(1)}, f32[4,128,768]{2,1,0:T(8,128)S(1)}, u32[]{:S(2)}, u32[]{:S(2)}) collective-permute-start(f32[4,128,768]{2,1,0:T(8,128)S(1)} %get-tuple-element.402), channel_id=1, source_target_pairs={{8,0},{16,8},{24,16},{32,24},{40,32},{48,40},{56,48},{64,56},{72,6... | collective-permute-start | bytes 4718600 | tf_op jit(solution)/shard_map/ppermute | solution.py:31
  546.8 13.7 %collective-permute-start.6 = (f32[4,512,128]{2,1,0:T(8,128)S(1)}, f32[4,512,128]{2,1,0:T(8,128)S(1)}, u32[]{:S(2)}, u32[]{:S(2)}) collective-permute-start(f32[4,512,128]{2,1,0:T(8,128)S(1)} %get-tuple-element.405), channel_id=1, source_target_pairs={{0,1},{1,2},{2,3},{3,4},{4,5},{5,6},{6,7},{8,9},{9,10},{10,11},{11... | collective-permute-start | bytes 3145736 | tf_op jit(solution)/shard_map/ppermute | solution.py:31
  548.7 16.1 %collective-permute-start.7 = (f32[4,512,128]{2,1,0:T(8,128)S(1)}, f32[4,512,128]{2,1,0:T(8,128)S(1)}, u32[]{:S(2)}, u32[]{:S(2)}) collective-permute-start(f32[4,512,128]{2,1,0:T(8,128)S(1)} %get-tuple-element.404), channel_id=1, source_target_pairs={{1,0},{2,1},{3,2},{4,3},{5,4},{6,5},{7,6},{9,8},{10,9},{11,10},{12... | collective-permute-start | bytes 3145736 | tf_op jit(solution)/shard_map/ppermute | solution.py:31
  560.6 4.2 copy-start.2
where the time goes:
time: 561 us; the launch traced here: 567 us
  starting transfers between devices  212 us (38%)
  matrix products  151 us (27%)
  waiting for transfers between devices  126 us (22%)
  local copies, waits for them, and re-layouts  43.3 us (8%)
  other arithmetic  19.2 us (3%)
  loops' own time  15.1 us (3%)
    ppermute x4, starting transfers between devices, shifted(): return lax.ppermute(block, axis, route)  200 us
    dot_general x96, matrix products, product(): jnp.dot(left, right, precision=HIGH, preferred_element_type=jnp.float32)  151 us
    ppermute x4, waiting for transfers between devices, shifted(): return lax.ppermute(block, axis, route)  81.6 us
    ppermute x2, waiting for transfers between devices, with_halo(): lax.ppermute(tail, axis, [(i, (i + 1) % count) for i in range(ends)])  35.3 us
    dynamic_update_slice x2, local copies, waits for them, and re-layouts, add_window(): lax.dynamic_update_slice(running, current + update, (anchor, row_start, c...  23.9 us
    another operation x1, loops' own time, shards(): summed = lax.fori_loop(0, own_count, own_step, summed)  15.1 us
  transfers between devices with their start and end apart: 8, of which 8 were waited for; matrix products, arithmetic and copies ran while one was open for 1% of the time, Pallas kernels for 0%

commit v1 on v0

v1 whole, which is shorter than its diff:
```python
import functools

import jax
import jax.numpy as jnp
import numpy as np
from jax import lax
from jax.experimental import pallas as pl
from jax.experimental.pallas import tpu as pltpu
from jax.sharding import PartitionSpec as P

F32 = jnp.float32
BF16 = jnp.bfloat16
MESH = pl.DeviceIdType.MESH
CHUNK = 64
COPIES = 14


def phase_tables(frame_len):
    half = frame_len // 2
    n = np.arange(half)[:, None]
    k = np.arange(half)[None, :]
    factor = 1.0 / np.sqrt(frame_len)
    even = 2.0 * np.pi * (n * 2 * k % frame_len) / frame_len
    odd = 2.0 * np.pi * (n * (2 * k + 1) % frame_len) / frame_len
    parts = [np.cos(even), np.sin(even), np.cos(odd), np.sin(odd), np.cos(odd).T, np.sin(odd).T]
    return np.stack([part * factor for part in parts]).astype(np.float32)


def split(value):
    high = value.astype(BF16)
    return high, (value - high.astype(F32)).astype(BF16)


def dot(left, right):
    return jnp.dot(left, right, preferred_element_type=F32)


def times(left_re, left_im, right_re, right_im):
    return left_re * right_re - left_im * right_im, left_re * right_im + left_im * right_re


def conj_times(left_re, left_im, right_re, right_im):
    return left_re * right_re + left_im * right_im, left_re * right_im - left_im * right_re


def kernel(
    n_gx, n_gy, offsets, counts, objects, probe_hbm, phase_hbm, intensity_hbm, tables_hbm, out,
    pad_one, pad_two, place_one, place_two, sum_one, sum_two, rows_one, rows_two, cols_one, cols_two,
    carry, second, gcarry, probe, wave, measured, raw, tables, phase, weights_r, weights_l, rows_in, cols_in,
    send_sem, recv_sem, local_sem, inner_sem,
):
    frame = probe.shape[1]
    half = frame // 2
    cap = intensity_hbm.shape[0]
    tile = objects.shape[1]
    ext = tile + frame
    low, high = half, half + tile
    gx, gy = lax.axis_index("gx"), lax.axis_index("gy")
    has_up, has_down = gx > 0, gx < n_gx - 1
    has_left, has_right = gy > 0, gy < n_gy - 1
    up, down, left, right = (gx - 1, gy), (gx + 1, gy), (gx, gy - 1), (gx, gy + 1)
    slices = ((pad_one, place_one, sum_one, rows_one, cols_one), (pad_two, place_two, sum_two, rows_two, cols_two))

    local = [
        pltpu.make_async_copy(tables_hbm, tables, local_sem.at[0]),
        pltpu.make_async_copy(phase_hbm, phase, local_sem.at[1]),
        pltpu.make_async_copy(intensity_hbm, raw, local_sem.at[2]),
        pltpu.make_async_copy(probe_hbm, probe, local_sem.at[3]),
    ]
    inner = [
        [
            pltpu.make_async_copy(
                objects.at[2 * which : 2 * which + 2, :, block * half : (block + 1) * half],
                pad.at[:, block + 1, low:high],
                inner_sem.at[which, block],
            )
            for block in range(tile // half)
        ]
        for which, pad in enumerate((pad_one, pad_two))
    ]
    local += inner[0] + inner[1]
    for copy in local:
        copy.start()

    barrier = pltpu.get_barrier_semaphore()
    sides = ((has_up, up), (has_down, down), (has_left, left), (has_right, right))
    for there, device in sides:

        @pl.when(there)
        def _():
            pl.semaphore_signal(barrier, inc=1, device_id=device, device_id_type=MESH)

    pl.semaphore_wait(barrier, sum(there.astype(jnp.int32) for there, _ in sides))

    def remote(number, source, target, device, sends, receives):
        copy = pltpu.make_async_remote_copy(
            src_ref=source, dst_ref=target, send_sem=send_sem.at[number], recv_sem=recv_sem.at[number],
            device_id=device, device_id_type=MESH,
        )
        return sends, receives, copy

    def start(copies):
        for sends, _, copy in copies:
            pl.when(sends)(copy.start)

    def wait_recv(copies):
        for _, receives, copy in copies:
            pl.when(receives)(copy.wait_recv)

    def wait_send(copies):
        for sends, _, copy in copies:
            pl.when(sends)(copy.wait_send)

    edge_pieces = (slice(0, half), slice(tile - half, tile))
    middle = slice(half, tile - half)

    def shift_by(piece, distance):
        return slice(piece.start + distance, piece.stop + distance)

    def halo(which):
        pad = slices[which][0]
        cells = objects.at[2 * which : 2 * which + 2]
        base = which * COPIES
        rows = []
        blocks = tile // half
        for block in (0, blocks - 1, *range(1, blocks - 1)):
            piece = slice(block * half, (block + 1) * half)
            rows.append(
                remote(base + len(rows), cells.at[:, 0:half, piece], pad.at[:, block + 1, high:ext], up, has_up, has_down)
            )
            rows.append(
                remote(base + len(rows), cells.at[:, tile - half : tile, piece], pad.at[:, block + 1, 0:low], down, has_down, has_up)
            )
        cols = [
            remote(base + 8, cells.at[:, :, 0:half], pad.at[:, blocks + 1, low:high], left, has_left, has_right),
            remote(base + 9, cells.at[:, :, tile - half : tile], pad.at[:, 0, low:high], right, has_right, has_left),
        ]
        corners = []
        for band, there in ((slice(0, low), has_up), (slice(high, ext), has_down)):
            to_left, to_right = jnp.logical_and(there, has_left), jnp.logical_and(there, has_right)
            corners.append(
                remote(base + 10 + len(corners), pad.at[:, 1, band], pad.at[:, blocks + 1, band], left, to_left, to_right)
            )
            corners.append(
                remote(base + 10 + len(corners), pad.at[:, blocks, band], pad.at[:, 0, band], right, to_right, to_left)
            )
        return rows, cols, corners

    def fold(which):
        _, _, total, land_rows, land_cols = slices[which]
        base = (2 + which) * COPIES
        rows = []
        for piece in (*edge_pieces, middle):
            moved = shift_by(piece, half)
            rows.append(
                remote(base + len(rows), total.at[:, 0:low, moved], land_rows.at[1, :, :, piece], up, has_up, has_down)
            )
            rows.append(
                remote(base + len(rows), total.at[:, high:ext, moved], land_rows.at[0, :, :, piece], down, has_down, has_up)
            )
        cols = [
            remote(base + 6, total.at[:, low:high, 0:low], land_cols.at[1, :, low:high], left, has_left, has_right),
            remote(base + 7, total.at[:, low:high, high:ext], land_cols.at[0, :, low:high], right, has_right, has_left),
        ]
        corners = []
        for band, there in ((slice(0, low), has_up), (slice(high, ext), has_down)):
            to_left, to_right = jnp.logical_and(there, has_left), jnp.logical_and(there, has_right)
            corners.append(
                remote(base + 8 + len(corners), total.at[:, band, 0:low], land_cols.at[1, :, band], left, to_left, to_right)
            )
            corners.append(
                remote(base + 8 + len(corners), total.at[:, band, high:ext], land_cols.at[0, :, band], right, to_right, to_left)
            )
        return rows, cols, corners

    halos = [halo(0), halo(1)]
    folds = [fold(0), fold(1)]

    start(halos[0][0] + halos[0][1])

    for pad in (pad_one, pad_two):

        @pl.when(jnp.logical_not(has_up))
        def _():
            pad[:, :, 0:low] = jnp.zeros((2, ext // half, low, half), F32)

        @pl.when(jnp.logical_not(has_down))
        def _():
            pad[:, :, high:ext] = jnp.zeros((2, ext // half, low, half), F32)

        @pl.when(jnp.logical_not(has_left))
        def _():
            pad[:, 0] = jnp.zeros((2, ext, half), F32)

        @pl.when(jnp.logical_not(has_right))
        def _():
            pad[:, ext // half - 1] = jnp.zeros((2, ext, half), F32)

    local[0].wait()
    cos_e, sin_e, cos_o, sin_o, cos_t, sin_t = (tables[i] for i in range(6))

    def real_form(cosine, sine):
        return jnp.concatenate([jnp.concatenate([cosine, -sine], 1), jnp.concatenate([sine, cosine], 1)], 0)

    forms = (real_form(cos_e, sin_e), real_form(cos_o, sin_o), real_form(cos_e, -sin_e), real_form(cos_t, -sin_t))
    for number, form in enumerate(forms):
        top, rest = split(form)
        for part, value in enumerate((top, top, rest)):
            weights_r[number, part * frame : (part + 1) * frame, :] = value
            weights_l[number, :, part * frame : (part + 1) * frame] = value

    place = lax.broadcasted_iota(jnp.int32, (frame, frame), 0)
    other = lax.broadcasted_iota(jnp.int32, (frame, frame), 1)

    def picked(i):
        return jnp.where(i < half, 2 * i, 2 * (i - half) + 1)

    pick_rows = jnp.where(other == picked(place), 1.0, 0.0).astype(BF16)
    pick_cols = jnp.where(place == picked(other), 1.0, 0.0).astype(BF16)

    def sorted_frequencies(value):
        for axis in (0, 1):
            top, rest = split(value)
            middle_part, last = split(value - top.astype(F32))
            del rest
            parts = (top, middle_part, last)
            if axis == 0:
                value = sum(dot(pick_rows, part) for part in parts[::-1])
            else:
                value = sum(dot(part, pick_cols) for part in parts[::-1])
        return value

    local[1].wait()
    angle = sorted_frequencies(phase[...])
    wave[0] = jnp.cos(angle)
    wave[1] = jnp.sin(angle)
    local[2].wait()

    def sort_slot(slot, nothing):
        measured[slot] = sorted_frequencies(raw[slot])
        return nothing

    lax.fori_loop(0, cap, sort_slot, 0)

    def clear_place(slot, nothing):
        for target in (place_one, place_two):
            for comp in range(2):
                target[comp, slot, 3] = jnp.zeros((4 * half, half), F32)
                for block in range(3):
                    target[comp, slot, block, 0:half] = jnp.zeros((half, half), F32)
                    target[comp, slot, block, 3 * half : 4 * half] = jnp.zeros((half, half), F32)
        return nothing

    lax.fori_loop(0, cap, clear_place, 0)
    local[3].wait()

    lane = lax.broadcasted_iota(jnp.int32, (CHUNK, half), 1)

    def column_of(slot):
        column = offsets[slot, 1]
        block = jnp.minimum(column // half, tile // half - 1)
        return block, column - block * half

    def window(pad, slot, comp, chunk):
        row = offsets[slot, 0]
        block, shift = column_of(slot)
        rows = pl.ds(row + chunk * CHUNK, CHUNK)
        back = jnp.where(jnp.logical_or(shift == 0, shift == half), 0, half - shift)
        turned = [pltpu.roll(pad[comp, block + i, rows, :], back, 1) for i in range(3)]
        kept = lane < half - shift
        return jnp.concatenate([jnp.where(kept, turned[i], turned[i + 1]) for i in range(2)], 1)

    def put(target, slot, comp, chunk, value):
        _, shift = column_of(slot)
        turn = jnp.where(shift == half, 0, shift)
        value = jnp.where(slot < counts[0], value, jnp.zeros_like(value))
        first = pltpu.roll(value[:, :half], turn, 1)
        last = pltpu.roll(value[:, half:], turn, 1)
        inside = lane >= shift
        nothing = jnp.zeros_like(first)
        rows = slice(half + chunk * CHUNK, half + (chunk + 1) * CHUNK)
        target[comp, slot, 0, rows] = jnp.where(inside, first, nothing)
        target[comp, slot, 1, rows] = jnp.where(inside, last, first)
        target[comp, slot, 2, rows] = jnp.where(inside, nothing, last)

    def right_dot(j, number):
        value = rows_in[j]
        return dot(jnp.concatenate([value, value[:, :frame]], 1), weights_r[number])

    def left_dot(i, number):
        value = cols_in[i]
        return dot(weights_l[number], jnp.concatenate([value, value[:frame]], 0))

    def there_and_back(before, between, after):
        chunks = [slice(c * CHUNK, (c + 1) * CHUNK) for c in range(frame // CHUNK)]
        for c, rows in enumerate(chunks):
            re, im = before(c, rows)
            for j in range(2):
                if j == 0:
                    mixed = jnp.concatenate([re[:, :half] + re[:, half:], im[:, :half] + im[:, half:]], 1)
                else:
                    mixed = jnp.concatenate([re[:, :half] - re[:, half:], im[:, :half] - im[:, half:]], 1)
                top, rest = split(mixed)
                rows_in[j, rows, 0:frame] = top
                rows_in[j, rows, frame : 2 * frame] = rest
        for j in range(2):
            value = right_dot(j, j)
            cols = slice(j * half, (j + 1) * half)
            for i in range(2):
                mixed = value[:half] + value[half:] if i == 0 else value[:half] - value[half:]
                for part, piece in enumerate(split(mixed)):
                    cols_in[i, part * frame : part * frame + half, cols] = piece[:, :half]
                    cols_in[i, part * frame + half : (part + 1) * frame, cols] = piece[:, half:]
        for i in range(2):
            value = left_dot(i, 2 + i)
            re, im = between(slice(i * half, (i + 1) * half), value[:half], value[half:])
            for position, field in enumerate((re, im)):
                for part, piece in enumerate(split(field)):
                    begin = part * frame + position * half
                    cols_in[i, begin : begin + half, :] = piece
        even, odd = left_dot(0, 0), left_dot(1, 1)
        for i in range(2):
            mixed = even + odd if i == 0 else even - odd
            rows = slice(i * half, (i + 1) * half)
            for j in range(2):
                for part, piece in enumerate(split(mixed[:, j * half : (j + 1) * half])):
                    begin = part * frame
                    rows_in[j, rows, begin : begin + half] = piece[:half]
                    rows_in[j, rows, begin + half : begin + frame] = piece[half:]
        even, odd = right_dot(0, 2), right_dot(1, 3)
        total, difference = even + odd, even - odd
        for c, rows in enumerate(chunks):
            re = jnp.concatenate([total[rows, :half], difference[rows, :half]], 1)
            im = jnp.concatenate([total[rows, half:], difference[rows, half:]], 1)
            after(c, rows, re, im)

    rows, cols, corners = halos[0]
    wait_recv(rows[:4])
    start(corners)
    wait_recv(rows[4:] + cols)
    start(halos[1][0] + halos[1][1])
    wait_recv(corners)
    for copy in inner[0]:
        copy.wait()

    def enter(slot, nothing):
        def before(chunk, rows):
            return times(probe[0, rows], probe[1, rows], window(pad_one, slot, 0, chunk), window(pad_one, slot, 1, chunk))

        def between(rows, re, im):
            return times(wave[0, rows], wave[1, rows], re, im)

        def after(chunk, rows, re, im):
            carry[slot, 0, rows] = re
            carry[slot, 1, rows] = im

        there_and_back(before, between, after)
        return nothing

    lax.fori_loop(0, cap, enter, 0)

    rows, cols, corners = halos[1]
    wait_recv(rows[:4])
    start(corners)
    wait_recv(rows[4:] + cols + corners)
    for copy in inner[1]:
        copy.wait()

    def leave(slot, nothing):
        def before(chunk, rows):
            second[slot, 0, rows] = window(pad_two, slot, 0, chunk)
            second[slot, 1, rows] = window(pad_two, slot, 1, chunk)
            return times(carry[slot, 0, rows], carry[slot, 1, rows], second[slot, 0, rows], second[slot, 1, rows])

        def between(rows, re, im):
            misfit = re * re + im * im - measured[slot, rows]
            return misfit * re, misfit * im

        def after(chunk, rows, re, im):
            two_re, two_im = conj_times(carry[slot, 0, rows], carry[slot, 1, rows], re, im)
            put(place_two, slot, 0, chunk, two_re)
            put(place_two, slot, 1, chunk, two_im)
            back_re, back_im = conj_times(second[slot, 0, rows], second[slot, 1, rows], re, im)
            gcarry[slot, 0, rows] = back_re
            gcarry[slot, 1, rows] = back_im

        there_and_back(before, between, after)
        return nothing

    lax.fori_loop(0, cap, leave, 0)

    blocks = ext // half

    def gather_block(which, row_block, col_block):
        _, target, total, _, _ = slices[which]
        for comp in range(2):
            value = None
            for slot in range(cap):
                block, _ = column_of(slot)
                moved = col_block - block
                taken = jnp.where(jnp.logical_and(moved >= 0, moved <= 2), moved, 3)
                begin = jnp.clip(row_block * half - offsets[slot, 0] + half, 0, 3 * half)
                piece = target[comp, slot, taken, pl.ds(begin, half), :]
                value = piece if value is None else value + piece
            rows = pl.ds(pl.multiple_of(row_block * half, half), half)
            cols = pl.ds(pl.multiple_of(col_block * half, half), half)
            total[comp, rows, cols] = value

    def gather_rows(which):
        def step(number, nothing):
            gather_block(which, (number // blocks) * (blocks - 1), number % blocks)
            return nothing

        lax.fori_loop(0, 2 * blocks, step, 0)

    def gather_cols(which):
        def step(number, nothing):
            gather_block(which, 1 + number // 2, (number % 2) * (blocks - 1))
            return nothing

        lax.fori_loop(0, 2 * (blocks - 2), step, 0)

    def gather_inner(which):
        def step(number, nothing):
            gather_block(which, 1 + number // (blocks - 2), 1 + number % (blocks - 2))
            return nothing

        lax.fori_loop(0, (blocks - 2) * (blocks - 2), step, 0)

    def send_sums(which):
        rows, cols, corners = folds[which]
        gather_rows(which)
        start(corners + rows[4:])
        gather_cols(which)
        start(cols)
        gather_inner(which)

    def pass_corners(which):
        rows, _, corners = folds[which]
        _, _, total, _, land_cols = slices[which]
        wait_recv(corners)
        for band, there in ((slice(0, low), has_up), (slice(high, ext), has_down)):
            for side, near, cell in ((0, has_left, slice(low, low + half)), (1, has_right, slice(high - half, high))):

                @pl.when(jnp.logical_and(there, near))
                def _():
                    for comp in range(2):
                        total[comp, band, cell] += land_cols[side, comp, band, :]

        start(rows[:4])

    def finish(which):
        rows, cols, corners = folds[which]
        _, _, total, land_rows, land_cols = slices[which]
        wait_recv(cols)
        for side, near, cell in ((0, has_left, slice(low, low + half)), (1, has_right, slice(high - half, high))):

            @pl.when(near)
            def _():
                for comp in range(2):
                    total[comp, low:high, cell] += land_cols[side, comp, low:high, :]

        wait_recv(rows)
        for side, near, cell in ((0, has_up, slice(low, low + half)), (1, has_down, slice(high - half, high))):

            @pl.when(near)
            def _():
                for comp in range(2):
                    total[comp, cell, low:high] += land_rows[side, comp]

        copy = pltpu.make_async_copy(
            total.at[:, low:high, low:high], out.at[2 * which : 2 * which + 2], local_sem.at[6 + which]
        )
        copy.start()
        return copy

    send_sums(1)

    def back(slot, nothing):
        def before(chunk, rows):
            return gcarry[slot, 0, rows], gcarry[slot, 1, rows]

        def between(rows, re, im):
            return conj_times(wave[0, rows], wave[1, rows], re, im)

        def after(chunk, rows, re, im):
            one_re, one_im = conj_times(probe[0, rows], probe[1, rows], re, im)
            put(place_one, slot, 0, chunk, one_re)
            put(place_one, slot, 1, chunk, one_im)

        there_and_back(before, between, after)

        @pl.when(slot == 1)
        def _():
            pass_corners(1)

        return nothing

    lax.fori_loop(0, cap, back, 0)

    send_sums(0)
    last = [finish(1)]
    pass_corners(0)
    last.append(finish(0))
    for exchange in halos + folds:
        for copies in exchange:
            wait_send(copies)
    for copy in last:
        copy.wait()


def shards(n_gx, n_gy, objects, probe_wave, prop_phase, intensity, offsets, counts):
    frame = intensity.shape[1]
    half = frame // 2
    cap = intensity.shape[0]
    tile = objects.shape[1]
    ext = tile + frame
    anywhere = pl.BlockSpec(memory_space=pl.ANY)
    scalars = pl.BlockSpec(memory_space=pltpu.SMEM)
    field = pltpu.VMEM((cap, 2, frame, frame), F32)
    scratch = [
        *[pltpu.VMEM((2, ext // half, ext, half), F32)] * 2,
        *[pltpu.VMEM((2, cap, 4, 4 * half, half), F32)] * 2,
        *[pltpu.VMEM((2, ext, ext), F32)] * 2,
        *[pltpu.VMEM((2, 2, half, tile), F32)] * 2,
        *[pltpu.VMEM((2, 2, ext, half), F32)] * 2,
        field,
        field,
        field,
        pltpu.VMEM((2, frame, frame), F32),
        pltpu.VMEM((2, frame, frame), F32),
        pltpu.VMEM((cap, frame, frame), F32),
        pltpu.VMEM((cap, frame, frame), F32),
        pltpu.VMEM((6, half, half), F32),
        pltpu.VMEM((frame, frame), F32),
        pltpu.VMEM((4, 3 * frame, frame), BF16),
        pltpu.VMEM((4, frame, 3 * frame), BF16),
        pltpu.VMEM((2, frame, 2 * frame), BF16),
        pltpu.VMEM((2, 2 * frame, frame), BF16),
        pltpu.SemaphoreType.DMA((4 * COPIES,)),
        pltpu.SemaphoreType.DMA((4 * COPIES,)),
        pltpu.SemaphoreType.DMA((8,)),
        pltpu.SemaphoreType.DMA((2, tile // half)),
    ]
    return pl.pallas_call(
        functools.partial(kernel, n_gx, n_gy),
        out_shape=jax.ShapeDtypeStruct(objects.shape, F32),
        in_specs=[scalars, scalars, *[anywhere] * 5],
        out_specs=anywhere,
        scratch_shapes=scratch,
        compiler_params=pltpu.CompilerParams(
            collective_id=0, has_side_effects=True, vmem_limit_bytes=60 * 1024 * 1024
        ),
        name="ptychography",
    )(offsets, counts, objects, probe_wave, prop_phase, intensity, jnp.asarray(phase_tables(frame)))


def solution(mesh):
    return jax.shard_map(
        functools.partial(shards, mesh.shape["gx"], mesh.shape["gy"]),
        mesh=mesh,
        in_specs=(
            P(None, "gx", "gy"),
            P(),
            P(),
            P(("gx", "gy"), None, None),
            P(("gx", "gy"), None),
            P(("gx", "gy")),
        ),
        out_specs=P(None, "gx", "gy"),
        check_vma=False,
    )
```

time: 561 us -> 76.3 us (0.14)
  the two profiles are of different devices: /device:TPU:79 before, /device:TPU:57 now
where the time goes in v1:
time: 76.3 us; the launch traced here: 76.1 us
  Pallas kernels  69.5 us (91%)
  local copies, waits for them, and re-layouts  5.98 us (8%)
    pallas_call x1, Pallas kernels, shards(): pl.pallas_call(functools.partial(kernel, n_gx, n_gy), out_shape=jax.Shape...  69.5 us
    unnamed x2, local copies, waits for them, and re-layouts  5.98 us

profile of v1, /device:TPU:57, one launch (start us, length us, event | category | flops | bytes accessed | tf_op | source)
XLA Modules:
  0.0 76.1 jit_solution(17410587286622245818)
XLA Ops:
  0.7 1.3 %copy.8.offsets = s32[4,2]{1,0:T(4,128)} copy(s32[4,2]{0,1:T(2,128)} %param.11) | data formatting | bytes 64 | tf_op args[4]
  2.0 69.5 %ptychography.1 = f32[4,512,512]{2,1,0:T(8,128)} custom-call(s32[4,2]{1,0:T(4,128)} %copy.8.offsets, s32[1]{0:T(128)S(6)} %copy.10.counts, f32[4,512,512]{2,1,0:T(8,128)} %objects.1, f32[2,256,256]{2,1,0:T(8,128)} %probe_hbm.1, f32[256,256]{1,0:T(8,128)} %phase_hbm.1, f32[4,256,256]{2,1,0:T(8,128)} %intensity_hbm.1, f32[6,128,128]{2,1,0:T(8,128)} %constant.2.clone.tables_hbm), custom_call_target="tpu_custom_call" | custom-call | tf_op jit(solution)/shard_map/ptychography/pallas_call | solution.py:545
  71.5 4.6 %copy.11 = f32[4,512,512]{2,1,0:T(8,128)} copy(f32[4,512,512]{2,1,0:T(8,128)} %ptychography.1) | data formatting | bytes 8388608

commit v2 on v1

--- a/solution.py
+++ b/solution.py
@@ -44,10 +44,10 @@
 
 
 def kernel(
-    n_gx, n_gy, offsets, counts, objects, probe_hbm, phase_hbm, intensity_hbm, tables_hbm, out,
+    n_gx, n_gy, offsets_hbm, counts_hbm, objects, probe_hbm, phase_hbm, intensity_hbm, tables_hbm, out,
     pad_one, pad_two, place_one, place_two, sum_one, sum_two, rows_one, rows_two, cols_one, cols_two,
     carry, second, gcarry, probe, wave, measured, raw, tables, phase, weights_r, weights_l, rows_in, cols_in,
-    send_sem, recv_sem, local_sem, inner_sem,
+    offsets, counts, send_sem, recv_sem, local_sem, inner_sem,
 ):
     frame = probe.shape[1]
     half = frame // 2
@@ -66,6 +66,8 @@
         pltpu.make_async_copy(phase_hbm, phase, local_sem.at[1]),
         pltpu.make_async_copy(intensity_hbm, raw, local_sem.at[2]),
         pltpu.make_async_copy(probe_hbm, probe, local_sem.at[3]),
+        pltpu.make_async_copy(offsets_hbm, offsets, local_sem.at[4]),
+        pltpu.make_async_copy(counts_hbm, counts, local_sem.at[5]),
     ]
     inner = [
         [
@@ -253,16 +255,18 @@
 
     lax.fori_loop(0, cap, clear_place, 0)
     local[3].wait()
+    local[4].wait()
+    local[5].wait()
 
     lane = lax.broadcasted_iota(jnp.int32, (CHUNK, half), 1)
 
     def column_of(slot):
-        column = offsets[slot, 1]
+        column = offsets[1, slot]
         block = jnp.minimum(column // half, tile // half - 1)
         return block, column - block * half
 
     def window(pad, slot, comp, chunk):
-        row = offsets[slot, 0]
+        row = offsets[0, slot]
         block, shift = column_of(slot)
         rows = pl.ds(row + chunk * CHUNK, CHUNK)
         back = jnp.where(jnp.logical_or(shift == 0, shift == half), 0, half - shift)
@@ -337,9 +341,8 @@
     rows, cols, corners = halos[0]
     wait_recv(rows[:4])
     start(corners)
-    wait_recv(rows[4:] + cols)
     start(halos[1][0] + halos[1][1])
-    wait_recv(corners)
+    wait_recv(rows[4:] + cols + corners)
     for copy in inner[0]:
         copy.wait()
 
@@ -399,7 +402,7 @@
                 block, _ = column_of(slot)
                 moved = col_block - block
                 taken = jnp.where(jnp.logical_and(moved >= 0, moved <= 2), moved, 3)
-                begin = jnp.clip(row_block * half - offsets[slot, 0] + half, 0, 3 * half)
+                begin = jnp.clip(row_block * half - offsets[0, slot] + half, 0, 3 * half)
                 piece = target[comp, slot, taken, pl.ds(begin, half), :]
                 value = piece if value is None else value + piece
             rows = pl.ds(pl.multiple_of(row_block * half, half), half)
@@ -499,8 +502,8 @@
     lax.fori_loop(0, cap, back, 0)
 
     send_sums(0)
+    pass_corners(0)
     last = [finish(1)]
-    pass_corners(0)
     last.append(finish(0))
     for exchange in halos + folds:
         for copies in exchange:
@@ -516,7 +519,6 @@
     tile = objects.shape[1]
     ext = tile + frame
     anywhere = pl.BlockSpec(memory_space=pl.ANY)
-    scalars = pl.BlockSpec(memory_space=pltpu.SMEM)
     field = pltpu.VMEM((cap, 2, frame, frame), F32)
     scratch = [
         *[pltpu.VMEM((2, ext // half, ext, half), F32)] * 2,
@@ -537,6 +539,8 @@
         pltpu.VMEM((4, frame, 3 * frame), BF16),
         pltpu.VMEM((2, frame, 2 * frame), BF16),
         pltpu.VMEM((2, 2 * frame, frame), BF16),
+        pltpu.SMEM((2, cap), jnp.int32),
+        pltpu.SMEM((1,), jnp.int32),
         pltpu.SemaphoreType.DMA((4 * COPIES,)),
         pltpu.SemaphoreType.DMA((4 * COPIES,)),
         pltpu.SemaphoreType.DMA((8,)),
@@ -545,14 +549,14 @@
     return pl.pallas_call(
         functools.partial(kernel, n_gx, n_gy),
         out_shape=jax.ShapeDtypeStruct(objects.shape, F32),
-        in_specs=[scalars, scalars, *[anywhere] * 5],
+        in_specs=[anywhere] * 7,
         out_specs=anywhere,
         scratch_shapes=scratch,
         compiler_params=pltpu.CompilerParams(
             collective_id=0, has_side_effects=True, vmem_limit_bytes=60 * 1024 * 1024
         ),
         name="ptychography",
-    )(offsets, counts, objects, probe_wave, prop_phase, intensity, jnp.asarray(phase_tables(frame)))
+    )(offsets.T, counts, objects, probe_wave, prop_phase, intensity, jnp.asarray(phase_tables(frame)))
 
 
 def solution(mesh):

time: 76.3 us -> 72.6 us (0.952)
  Pallas kernels: 69.5 us -> 67.1 us
  local copies, waits for them, and re-layouts: 5.98 us -> 4.64 us
    pallas_call x1, Pallas kernels: 69.5 us -> 67.1 us  [shards(): pl.pallas_call(functools.partial(kernel, n_gx, n_gy), out_shape=jax.Shape...]
    unnamed x2 -> x1, local copies, waits for them, and re-layouts: 5.98 us -> 4.64 us
where the time goes in v2:
time: 72.6 us; the launch traced here: 72.4 us
  Pallas kernels  67.1 us (92%)
  local copies, waits for them, and re-layouts  4.64 us (6%)
    pallas_call x1, Pallas kernels, shards(): pl.pallas_call(functools.partial(kernel, n_gx, n_gy), out_shape=jax.Shape...  67.1 us
    unnamed x1, local copies, waits for them, and re-layouts  4.64 us

profile of v2, /device:TPU:57, one launch (start us, length us, event | category | flops | bytes accessed | tf_op | source)
XLA Modules:
  0.0 72.4 jit_solution(4333508514109510967)
XLA Ops:
  0.7 67.1 %ptychography.1 = f32[4,512,512]{2,1,0:T(8,128)} custom-call(s32[2,4]{1,0:T(2,128)} %bitcast.1, s32[1]{0:T(128)S(6)} %copy.9.counts_hbm, f32[4,512,512]{2,1,0:T(8,128)} %objects.1, f32[2,256,256]{2,1,0:T(8,128)} %probe_hbm.1, f32[256,256]{1,0:T(8,128)} %phase_hbm.1, f32[4,256,256]{2,1,0:T(8,128)} %intensity_hbm.1, f32[6,128,128]{2,1,0:T(8,128)} %constant.2.clone.tables_hbm), custom_call_target="tpu_custom_call" | custom-call | tf_op jit(solution)/shard_map/ptychography/pallas_call | solution.py:549
  67.8 4.6 %copy.10 = f32[4,512,512]{2,1,0:T(8,128)} copy(f32[4,512,512]{2,1,0:T(8,128)} %ptychography.1) | data formatting | bytes 8388608

commit v3 on v2

--- a/solution.py
+++ b/solution.py
@@ -13,6 +13,8 @@
 MESH = pl.DeviceIdType.MESH
 CHUNK = 64
 COPIES = 14
+GROUP = 2
+steps_end = object()
 
 
 def phase_tables(frame_len):
@@ -45,8 +47,8 @@
 
 def kernel(
     n_gx, n_gy, offsets_hbm, counts_hbm, objects, probe_hbm, phase_hbm, intensity_hbm, tables_hbm, out,
-    pad_one, pad_two, place_one, place_two, sum_one, sum_two, rows_one, rows_two, cols_one, cols_two,
-    carry, second, gcarry, probe, wave, measured, raw, tables, phase, weights_r, weights_l, rows_in, cols_in,
+    pad_one, pad_two, place_one, place_two, top_one, top_two, side_one, side_two, rows_one, rows_two, cols_one, cols_two,
+    carry, second, probe, wave, measured, tables, phase, weights_r, weights_l, rows_in, cols_in,
     offsets, counts, send_sem, recv_sem, local_sem, inner_sem,
 ):
     frame = probe.shape[1]
@@ -59,12 +61,15 @@
     has_up, has_down = gx > 0, gx < n_gx - 1
     has_left, has_right = gy > 0, gy < n_gy - 1
     up, down, left, right = (gx - 1, gy), (gx + 1, gy), (gx, gy - 1), (gx, gy + 1)
-    slices = ((pad_one, place_one, sum_one, rows_one, cols_one), (pad_two, place_two, sum_two, rows_two, cols_two))
+    slices = (
+        (pad_one, place_one, top_one, side_one, rows_one, cols_one),
+        (pad_two, place_two, top_two, side_two, rows_two, cols_two),
+    )
 
     local = [
         pltpu.make_async_copy(tables_hbm, tables, local_sem.at[0]),
         pltpu.make_async_copy(phase_hbm, phase, local_sem.at[1]),
-        pltpu.make_async_copy(intensity_hbm, raw, local_sem.at[2]),
+        pltpu.make_async_copy(intensity_hbm, measured, local_sem.at[2]),
         pltpu.make_async_copy(probe_hbm, probe, local_sem.at[3]),
         pltpu.make_async_copy(offsets_hbm, offsets, local_sem.at[4]),
         pltpu.make_async_copy(counts_hbm, counts, local_sem.at[5]),
@@ -149,29 +154,29 @@
         return rows, cols, corners
 
     def fold(which):
-        _, _, total, land_rows, land_cols = slices[which]
+        _, _, top, side, land_rows, land_cols = slices[which]
         base = (2 + which) * COPIES
         rows = []
         for piece in (*edge_pieces, middle):
             moved = shift_by(piece, half)
             rows.append(
-                remote(base + len(rows), total.at[:, 0:low, moved], land_rows.at[1, :, :, piece], up, has_up, has_down)
+                remote(base + len(rows), top.at[:, 0, :, moved], land_rows.at[1, :, :, piece], up, has_up, has_down)
             )
             rows.append(
-                remote(base + len(rows), total.at[:, high:ext, moved], land_rows.at[0, :, :, piece], down, has_down, has_up)
+                remote(base + len(rows), top.at[:, 1, :, moved], land_rows.at[0, :, :, piece], down, has_down, has_up)
             )
         cols = [
-            remote(base + 6, total.at[:, low:high, 0:low], land_cols.at[1, :, low:high], left, has_left, has_right),
-            remote(base + 7, total.at[:, low:high, high:ext], land_cols.at[0, :, low:high], right, has_right, has_left),
+            remote(base + 6, side.at[:, 0], land_cols.at[1, :, low:high], left, has_left, has_right),
+            remote(base + 7, side.at[:, 1], land_cols.at[0, :, low:high], right, has_right, has_left),
         ]
         corners = []
-        for band, there in ((slice(0, low), has_up), (slice(high, ext), has_down)):
+        for edge, band, there in ((0, slice(0, low), has_up), (1, slice(high, ext), has_down)):
             to_left, to_right = jnp.logical_and(there, has_left), jnp.logical_and(there, has_right)
             corners.append(
-                remote(base + 8 + len(corners), total.at[:, band, 0:low], land_cols.at[1, :, band], left, to_left, to_right)
+                remote(base + 8 + len(corners), top.at[:, edge, :, 0:low], land_cols.at[1, :, band], left, to_left, to_right)
             )
             corners.append(
-                remote(base + 8 + len(corners), total.at[:, band, high:ext], land_cols.at[0, :, band], right, to_right, to_left)
+                remote(base + 8 + len(corners), top.at[:, edge, :, high:ext], land_cols.at[0, :, band], right, to_right, to_left)
             )
         return rows, cols, corners
 
@@ -239,10 +244,15 @@
     local[2].wait()
 
     def sort_slot(slot, nothing):
-        measured[slot] = sorted_frequencies(raw[slot])
+        measured[slot] = sorted_frequencies(measured[slot])
         return nothing
 
     lax.fori_loop(0, cap, sort_slot, 0)
+
+    rows, cols, corners = halos[0]
+    wait_recv(rows[:4])
+    start(corners)
+    start(halos[1][0] + halos[1][1])
 
     def clear_place(slot, nothing):
         for target in (place_one, place_two):
@@ -287,15 +297,15 @@
         target[comp, slot, 1, rows] = jnp.where(inside, last, first)
         target[comp, slot, 2, rows] = jnp.where(inside, nothing, last)
 
-    def right_dot(j, number):
-        value = rows_in[j]
+    def right_dot(lane_of, j, number):
+        value = rows_in[lane_of, j]
         return dot(jnp.concatenate([value, value[:, :frame]], 1), weights_r[number])
 
-    def left_dot(i, number):
-        value = cols_in[i]
+    def left_dot(lane_of, i, number):
+        value = cols_in[lane_of, i]
         return dot(weights_l[number], jnp.concatenate([value, value[:frame]], 0))
 
-    def there_and_back(before, between, after):
+    def there_and_back(which, before, between, after):
         chunks = [slice(c * CHUNK, (c + 1) * CHUNK) for c in range(frame // CHUNK)]
         for c, rows in enumerate(chunks):
             re, im = before(c, rows)
@@ -305,48 +315,62 @@
                 else:
                     mixed = jnp.concatenate([re[:, :half] - re[:, half:], im[:, :half] - im[:, half:]], 1)
                 top, rest = split(mixed)
-                rows_in[j, rows, 0:frame] = top
-                rows_in[j, rows, frame : 2 * frame] = rest
+                rows_in[which, j, rows, 0:frame] = top
+                rows_in[which, j, rows, frame : 2 * frame] = rest
+        yield
         for j in range(2):
-            value = right_dot(j, j)
+            value = right_dot(which, j, j)
             cols = slice(j * half, (j + 1) * half)
             for i in range(2):
                 mixed = value[:half] + value[half:] if i == 0 else value[:half] - value[half:]
                 for part, piece in enumerate(split(mixed)):
-                    cols_in[i, part * frame : part * frame + half, cols] = piece[:, :half]
-                    cols_in[i, part * frame + half : (part + 1) * frame, cols] = piece[:, half:]
+                    cols_in[which, i, part * frame : part * frame + half, cols] = piece[:, :half]
+                    cols_in[which, i, part * frame + half : (part + 1) * frame, cols] = piece[:, half:]
+        yield
         for i in range(2):
-            value = left_dot(i, 2 + i)
+            value = left_dot(which, i, 2 + i)
             re, im = between(slice(i * half, (i + 1) * half), value[:half], value[half:])
             for position, field in enumerate((re, im)):
                 for part, piece in enumerate(split(field)):
                     begin = part * frame + position * half
-                    cols_in[i, begin : begin + half, :] = piece
-        even, odd = left_dot(0, 0), left_dot(1, 1)
+                    cols_in[which, i, begin : begin + half, :] = piece
+        yield
+        even, odd = left_dot(which, 0, 0), left_dot(which, 1, 1)
         for i in range(2):
             mixed = even + odd if i == 0 else even - odd
             rows = slice(i * half, (i + 1) * half)
             for j in range(2):
                 for part, piece in enumerate(split(mixed[:, j * half : (j + 1) * half])):
                     begin = part * frame
-                    rows_in[j, rows, begin : begin + half] = piece[:half]
-                    rows_in[j, rows, begin + half : begin + frame] = piece[half:]
-        even, odd = right_dot(0, 2), right_dot(1, 3)
+                    rows_in[which, j, rows, begin : begin + half] = piece[:half]
+                    rows_in[which, j, rows, begin + half : begin + frame] = piece[half:]
+        yield
+        even, odd = right_dot(which, 0, 2), right_dot(which, 1, 3)
         total, difference = even + odd, even - odd
         for c, rows in enumerate(chunks):
             re = jnp.concatenate([total[rows, :half], difference[rows, :half]], 1)
             im = jnp.concatenate([total[rows, half:], difference[rows, half:]], 1)
             after(c, rows, re, im)
 
-    rows, cols, corners = halos[0]
-    wait_recv(rows[:4])
-    start(corners)
-    start(halos[1][0] + halos[1][1])
+    def frames(steps_of, then=None):
+        def group(number, nothing):
+            waiting = [steps_of(which, number * GROUP + which) for which in range(GROUP)]
+            running = []
+            while waiting or running:
+                if waiting:
+                    running.append(waiting.pop(0))
+                running = [steps for steps in running if next(steps, steps_end) is not steps_end]
+            if then is not None:
+                then(number)
+            return nothing
+
+        lax.fori_loop(0, cap // GROUP, group, 0)
+
     wait_recv(rows[4:] + cols + corners)
     for copy in inner[0]:
         copy.wait()
 
-    def enter(slot, nothing):
+    def enter(which, slot):
         def before(chunk, rows):
             return times(probe[0, rows], probe[1, rows], window(pad_one, slot, 0, chunk), window(pad_one, slot, 1, chunk))
 
@@ -357,10 +381,9 @@
             carry[slot, 0, rows] = re
             carry[slot, 1, rows] = im
 
-        there_and_back(before, between, after)
-        return nothing
-
-    lax.fori_loop(0, cap, enter, 0)
+        return there_and_back(which, before, between, after)
+
+    frames(enter)
 
     rows, cols, corners = halos[1]
     wait_recv(rows[:4])
@@ -369,7 +392,7 @@
     for copy in inner[1]:
         copy.wait()
 
-    def leave(slot, nothing):
+    def leave(which, slot):
         def before(chunk, rows):
             second[slot, 0, rows] = window(pad_two, slot, 0, chunk)
             second[slot, 1, rows] = window(pad_two, slot, 1, chunk)
@@ -384,104 +407,115 @@
             put(place_two, slot, 0, chunk, two_re)
             put(place_two, slot, 1, chunk, two_im)
             back_re, back_im = conj_times(second[slot, 0, rows], second[slot, 1, rows], re, im)
-            gcarry[slot, 0, rows] = back_re
-            gcarry[slot, 1, rows] = back_im
-
-        there_and_back(before, between, after)
-        return nothing
-
-    lax.fori_loop(0, cap, leave, 0)
+            second[slot, 0, rows] = back_re
+            second[slot, 1, rows] = back_im
+
+        return there_and_back(which, before, between, after)
+
+    frames(leave)
 
     blocks = ext // half
-
-    def gather_block(which, row_block, col_block):
-        _, target, total, _, _ = slices[which]
-        for comp in range(2):
-            value = None
-            for slot in range(cap):
-                block, _ = column_of(slot)
-                moved = col_block - block
-                taken = jnp.where(jnp.logical_and(moved >= 0, moved <= 2), moved, 3)
-                begin = jnp.clip(row_block * half - offsets[0, slot] + half, 0, 3 * half)
-                piece = target[comp, slot, taken, pl.ds(begin, half), :]
-                value = piece if value is None else value + piece
-            rows = pl.ds(pl.multiple_of(row_block * half, half), half)
-            cols = pl.ds(pl.multiple_of(col_block * half, half), half)
-            total[comp, rows, cols] = value
-
-    def gather_rows(which):
+    last = blocks - 1
+
+    def gathered(which, comp, row_block, col_block):
+        target = slices[which][1]
+        value = None
+        for slot in range(cap):
+            block, _ = column_of(slot)
+            moved = col_block - block
+            taken = jnp.where(jnp.logical_and(moved >= 0, moved <= 2), moved, 3)
+            begin = jnp.clip(row_block * half - offsets[0, slot] + half, 0, 3 * half)
+            piece = target[comp, slot, taken, pl.ds(begin, half), :]
+            value = piece if value is None else value + piece
+        return value
+
+    def block_at(number):
+        return pl.ds(pl.multiple_of(number * half, half), half)
+
+    def gather_top(which, first_col, step_col):
+        top = slices[which][2]
+
         def step(number, nothing):
-            gather_block(which, (number // blocks) * (blocks - 1), number % blocks)
+            edge, col_block = number // 2, first_col + number % 2 * step_col
+            for comp in range(2):
+                top[comp, edge, :, block_at(col_block)] = gathered(which, comp, edge * last, col_block)
             return nothing
 
-        lax.fori_loop(0, 2 * blocks, step, 0)
-
-    def gather_cols(which):
+        lax.fori_loop(0, 4, step, 0)
+
+    def gather_sides(which):
+        side = slices[which][3]
+
         def step(number, nothing):
-            gather_block(which, 1 + number // 2, (number % 2) * (blocks - 1))
+            near, row_block = number % 2, number // 2
+            for comp in range(2):
+                side[comp, near, block_at(row_block), :] = gathered(which, comp, row_block + 1, near * last)
             return nothing
 
         lax.fori_loop(0, 2 * (blocks - 2), step, 0)
 
     def gather_inner(which):
         def step(number, nothing):
-            gather_block(which, 1 + number // (blocks - 2), 1 + number % (blocks - 2))
+            row_block, col_block = number // (blocks - 2), number % (blocks - 2)
+            for comp in range(2):
+                out[2 * which + comp, block_at(row_block), block_at(col_block)] = gathered(
+                    which, comp, row_block + 1, col_block + 1
+                )
             return nothing
 
         lax.fori_loop(0, (blocks - 2) * (blocks - 2), step, 0)
 
     def send_sums(which):
         rows, cols, corners = folds[which]
-        gather_rows(which)
-        start(corners + rows[4:])
-        gather_cols(which)
+        gather_top(which, 0, last)
+        start(corners)
+        gather_top(which, 2, 1)
+        start(rows[4:])
+        gather_top(which, 1, last - 2)
+        gather_sides(which)
         start(cols)
         gather_inner(which)
 
     def pass_corners(which):
         rows, _, corners = folds[which]
-        _, _, total, _, land_cols = slices[which]
+        _, _, top, _, _, land_cols = slices[which]
         wait_recv(corners)
-        for band, there in ((slice(0, low), has_up), (slice(high, ext), has_down)):
+        for edge, band, there in ((0, slice(0, low), has_up), (1, slice(high, ext), has_down)):
             for side, near, cell in ((0, has_left, slice(low, low + half)), (1, has_right, slice(high - half, high))):
 
                 @pl.when(jnp.logical_and(there, near))
                 def _():
                     for comp in range(2):
-                        total[comp, band, cell] += land_cols[side, comp, band, :]
+                        top[comp, edge, :, cell] += land_cols[side, comp, band, :]
 
         start(rows[:4])
 
     def finish(which):
-        rows, cols, corners = folds[which]
-        _, _, total, land_rows, land_cols = slices[which]
+        rows, cols, _ = folds[which]
+        _, _, _, _, land_rows, land_cols = slices[which]
         wait_recv(cols)
-        for side, near, cell in ((0, has_left, slice(low, low + half)), (1, has_right, slice(high - half, high))):
+        for side, near, cell in ((0, has_left, edge_pieces[0]), (1, has_right, edge_pieces[1])):
 
             @pl.when(near)
             def _():
                 for comp in range(2):
-                    total[comp, low:high, cell] += land_cols[side, comp, low:high, :]
-
-        wait_recv(rows)
-        for side, near, cell in ((0, has_up, slice(low, low + half)), (1, has_down, slice(high - half, high))):
-
-            @pl.when(near)
-            def _():
-                for comp in range(2):
-                    total[comp, cell, low:high] += land_rows[side, comp]
-
-        copy = pltpu.make_async_copy(
-            total.at[:, low:high, low:high], out.at[2 * which : 2 * which + 2], local_sem.at[6 + which]
-        )
-        copy.start()
-        return copy
+                    out[2 * which + comp, :, cell] += land_cols[side, comp, low:high, :]
+
+        for arrived, pieces in ((rows[4:], (middle,)), (rows[:4], edge_pieces)):
+            wait_recv(arrived)
+            for side, near, cell in ((0, has_up, edge_pieces[0]), (1, has_down, edge_pieces[1])):
+
+                @pl.when(near)
+                def _():
+                    for comp in range(2):
+                        for piece in pieces:
+                            out[2 * which + comp, cell, piece] += land_rows[side, comp, :, piece]
 
     send_sums(1)
 
-    def back(slot, nothing):
+    def back(which, slot):
         def before(chunk, rows):
-            return gcarry[slot, 0, rows], gcarry[slot, 1, rows]
+            return second[slot, 0, rows], second[slot, 1, rows]
 
         def between(rows, re, im):
             return conj_times(wave[0, rows], wave[1, rows], re, im)
@@ -491,25 +525,22 @@
             put(place_one, slot, 0, chunk, one_re)
             put(place_one, slot, 1, chunk, one_im)
 
-        there_and_back(before, between, after)
-
-        @pl.when(slot == 1)
+        return there_and_back(which, before, between, after)
+
+    def between_groups(number):
+        @pl.when(number == 0)
         def _():
             pass_corners(1)
 
-        return nothing
-
-    lax.fori_loop(0, cap, back, 0)
+    frames(back, between_groups)
 
     send_sums(0)
     pass_corners(0)
-    last = [finish(1)]
-    last.append(finish(0))
+    finish(1)
+    finish(0)
     for exchange in halos + folds:
         for copies in exchange:
             wait_send(copies)
-    for copy in last:
-        copy.wait()
 
 
 def shards(n_gx, n_gy, objects, probe_wave, prop_phase, intensity, offsets, counts):
@@ -523,22 +554,21 @@
     scratch = [
         *[pltpu.VMEM((2, ext // half, ext, half), F32)] * 2,
         *[pltpu.VMEM((2, cap, 4, 4 * half, half), F32)] * 2,
-        *[pltpu.VMEM((2, ext, ext), F32)] * 2,
+        *[pltpu.VMEM((2, 2, half, ext), F32)] * 2,
+        *[pltpu.VMEM((2, 2, tile, half), F32)] * 2,
         *[pltpu.VMEM((2, 2, half, tile), F32)] * 2,
         *[pltpu.VMEM((2, 2, ext, half), F32)] * 2,
-        field,
         field,
         field,
         pltpu.VMEM((2, frame, frame), F32),
         pltpu.VMEM((2, frame, frame), F32),
         pltpu.VMEM((cap, frame, frame), F32),
-        pltpu.VMEM((cap, frame, frame), F32),
         pltpu.VMEM((6, half, half), F32),
         pltpu.VMEM((frame, frame), F32),
         pltpu.VMEM((4, 3 * frame, frame), BF16),
         pltpu.VMEM((4, frame, 3 * frame), BF16),
-        pltpu.VMEM((2, frame, 2 * frame), BF16),
-        pltpu.VMEM((2, 2 * frame, frame), BF16),
+        pltpu.VMEM((GROUP, 2, frame, 2 * frame), BF16),
+        pltpu.VMEM((GROUP, 2, 2 * frame, frame), BF16),
         pltpu.SMEM((2, cap), jnp.int32),
         pltpu.SMEM((1,), jnp.int32),
         pltpu.SemaphoreType.DMA((4 * COPIES,)),
@@ -548,12 +578,12 @@
     ]
     return pl.pallas_call(
         functools.partial(kernel, n_gx, n_gy),
-        out_shape=jax.ShapeDtypeStruct(objects.shape, F32),
+        out_shape=pltpu.VMEM(objects.shape, F32),
         in_specs=[anywhere] * 7,
-        out_specs=anywhere,
+        out_specs=pl.BlockSpec(memory_space=pltpu.VMEM),
         scratch_shapes=scratch,
         compiler_params=pltpu.CompilerParams(
-            collective_id=0, has_side_effects=True, vmem_limit_bytes=60 * 1024 * 1024
+            collective_id=0, has_side_effects=True, vmem_limit_bytes=58 * 1024 * 1024
         ),
         name="ptychography",
     )(offsets.T, counts, objects, probe_wave, prop_phase, intensity, jnp.asarray(phase_tables(frame)))

time: 72.6 us -> 64.4 us (0.89)
  Pallas kernels: 67.1 us -> 61.6 us
  local copies, waits for them, and re-layouts: 4.64 us -> 2.02 us
    pallas_call x1, Pallas kernels: 67.1 us -> 61.6 us  [shards(): pl.pallas_call(functools.partial(kernel, n_gx, n_gy), out_shape=pltpu.VME...]
    unnamed x1, local copies, waits for them, and re-layouts: 4.64 us -> 2.02 us
where the time goes in v3:
time: 64.4 us; the launch traced here: 64.3 us
  Pallas kernels  61.6 us (96%)
  local copies, waits for them, and re-layouts  2.02 us (3%)
  between operations  0.66 us (1%)
    pallas_call x1, Pallas kernels, shards(): pl.pallas_call(functools.partial(kernel, n_gx, n_gy), out_shape=pltpu.VME...  61.6 us
    unnamed x1, local copies, waits for them, and re-layouts  2.02 us

profile of v3, /device:TPU:57, one launch (start us, length us, event | category | flops | bytes accessed | tf_op | source)
XLA Modules:
  0.0 64.3 jit_solution(13933407521786965306)
XLA Ops:
  0.7 61.6 %ptychography.1 = f32[4,512,512]{2,1,0:T(8,128)S(1)} custom-call(s32[2,4]{1,0:T(2,128)} %bitcast.1, s32[1]{0:T(128)S(6)} %copy.10.counts_hbm, f32[4,512,512]{2,1,0:T(8,128)} %objects.1, f32[2,256,256]{2,1,0:T(8,128)} %probe_hbm.1, f32[256,256]{1,0:T(8,128)} %phase_hbm.1, f32[4,256,256]{2,1,0:T(8,128)} %intensity_hbm.1, f32[6,128,128]{2,1,0:T(8,128)} %constant.2.clone.tables_hbm), custom_call_target="tpu_custom_call" | custom-call | tf_op jit(solution)/shard_map/ptychography/pallas_call | solution.py:579
  62.2 2.0 %copy.9 = f32[4,512,512]{2,1,0:T(8,128)} copy(f32[4,512,512]{2,1,0:T(8,128)S(1)} %ptychography.1) | data formatting | bytes 8388608

commit v4 on v3

--- a/solution.py
+++ b/solution.py
@@ -48,7 +48,7 @@
 def kernel(
     n_gx, n_gy, offsets_hbm, counts_hbm, objects, probe_hbm, phase_hbm, intensity_hbm, tables_hbm, out,
     pad_one, pad_two, place_one, place_two, top_one, top_two, side_one, side_two, rows_one, rows_two, cols_one, cols_two,
-    carry, second, probe, wave, measured, tables, phase, weights_r, weights_l, rows_in, cols_in,
+    carry, second, gexit, probe, wave, measured, tables, phase, weights_r, weights_l, rows_in, cols_in,
     offsets, counts, send_sem, recv_sem, local_sem, inner_sem,
 ):
     frame = probe.shape[1]
@@ -183,7 +183,8 @@
     halos = [halo(0), halo(1)]
     folds = [fold(0), fold(1)]
 
-    start(halos[0][0] + halos[0][1])
+    (rows_a, cols_a, corners_a), (rows_b, cols_b, corners_b) = halos
+    start(rows_a[:4] + rows_b[:4] + cols_a)
 
     for pad in (pad_one, pad_two):
 
@@ -241,6 +242,8 @@
     angle = sorted_frequencies(phase[...])
     wave[0] = jnp.cos(angle)
     wave[1] = jnp.sin(angle)
+    wait_send(rows_a[:4])
+    start(rows_a[4:] + cols_b)
     local[2].wait()
 
     def sort_slot(slot, nothing):
@@ -249,10 +252,8 @@
 
     lax.fori_loop(0, cap, sort_slot, 0)
 
-    rows, cols, corners = halos[0]
-    wait_recv(rows[:4])
-    start(corners)
-    start(halos[1][0] + halos[1][1])
+    wait_recv(rows_a[:4])
+    start(corners_a)
 
     def clear_place(slot, nothing):
         for target in (place_one, place_two):
@@ -354,11 +355,8 @@
 
     def frames(steps_of, then=None):
         def group(number, nothing):
-            waiting = [steps_of(which, number * GROUP + which) for which in range(GROUP)]
-            running = []
-            while waiting or running:
-                if waiting:
-                    running.append(waiting.pop(0))
+            running = [steps_of(which, number * GROUP + which) for which in range(GROUP)]
+            while running:
                 running = [steps for steps in running if next(steps, steps_end) is not steps_end]
             if then is not None:
                 then(number)
@@ -366,7 +364,9 @@
 
         lax.fori_loop(0, cap // GROUP, group, 0)
 
-    wait_recv(rows[4:] + cols + corners)
+    wait_recv(rows_b[:4])
+    start(corners_b + rows_b[4:])
+    wait_recv(rows_a[4:] + cols_a + corners_a)
     for copy in inner[0]:
         copy.wait()
 
@@ -385,10 +385,7 @@
 
     frames(enter)
 
-    rows, cols, corners = halos[1]
-    wait_recv(rows[:4])
-    start(corners)
-    wait_recv(rows[4:] + cols + corners)
+    wait_recv(rows_b[4:] + cols_b + corners_b)
     for copy in inner[1]:
         copy.wait()
 
@@ -406,9 +403,8 @@
             two_re, two_im = conj_times(carry[slot, 0, rows], carry[slot, 1, rows], re, im)
             put(place_two, slot, 0, chunk, two_re)
             put(place_two, slot, 1, chunk, two_im)
-            back_re, back_im = conj_times(second[slot, 0, rows], second[slot, 1, rows], re, im)
-            second[slot, 0, rows] = back_re
-            second[slot, 1, rows] = back_im
+            gexit[slot, 0, rows] = re
+            gexit[slot, 1, rows] = im
 
         return there_and_back(which, before, between, after)
 
@@ -515,7 +511,7 @@
 
     def back(which, slot):
         def before(chunk, rows):
-            return second[slot, 0, rows], second[slot, 1, rows]
+            return conj_times(second[slot, 0, rows], second[slot, 1, rows], gexit[slot, 0, rows], gexit[slot, 1, rows])
 
         def between(rows, re, im):
             return conj_times(wave[0, rows], wave[1, rows], re, im)
@@ -538,7 +534,8 @@
     pass_corners(0)
     finish(1)
     finish(0)
-    for exchange in halos + folds:
+    wait_send(rows_a[4:] + cols_a + corners_a)
+    for exchange in [halos[1], *folds]:
         for copies in exchange:
             wait_send(copies)
 
@@ -558,6 +555,7 @@
         *[pltpu.VMEM((2, 2, tile, half), F32)] * 2,
         *[pltpu.VMEM((2, 2, half, tile), F32)] * 2,
         *[pltpu.VMEM((2, 2, ext, half), F32)] * 2,
+        field,
         field,
         field,
         pltpu.VMEM((2, frame, frame), F32),

time: 64.4 us -> 62.5 us (0.970)
  Pallas kernels: 61.6 us -> 59.3 us
    pallas_call x1, Pallas kernels: 61.6 us -> 59.3 us  [shards(): pl.pallas_call(functools.partial(kernel, n_gx, n_gy), out_shape=pltpu.VME...]
where the time goes in v4:
time: 62.5 us; the launch traced here: 62 us
  Pallas kernels  59.3 us (95%)
  local copies, waits for them, and re-layouts  2.02 us (3%)
  between operations  0.66 us (1%)
    pallas_call x1, Pallas kernels, shards(): pl.pallas_call(functools.partial(kernel, n_gx, n_gy), out_shape=pltpu.VME...  59.3 us
    unnamed x1, local copies, waits for them, and re-layouts  2.02 us

profile of v4, /device:TPU:57, one launch (start us, length us, event | category | flops | bytes accessed | tf_op | source)
XLA Modules:
  0.0 62.0 jit_solution(16391710535571624302)
XLA Ops:
  0.7 59.3 %ptychography.1 = f32[4,512,512]{2,1,0:T(8,128)S(1)} custom-call(s32[2,4]{1,0:T(2,128)} %bitcast.1, s32[1]{0:T(128)S(6)} %copy.10.counts_hbm, f32[4,512,512]{2,1,0:T(8,128)} %objects.1, f32[2,256,256]{2,1,0:T(8,128)} %probe_hbm.1, f32[256,256]{1,0:T(8,128)} %phase_hbm.1, f32[4,256,256]{2,1,0:T(8,128)} %intensity_hbm.1, f32[6,128,128]{2,1,0:T(8,128)} %constant.2.clone.tables_hbm), custom_call_target="tpu_custom_call" | custom-call | tf_op jit(solution)/shard_map/ptychography/pallas_call | solution.py:577
  60.0 2.0 %copy.9 = f32[4,512,512]{2,1,0:T(8,128)} copy(f32[4,512,512]{2,1,0:T(8,128)S(1)} %ptychography.1) | data formatting | bytes 8388608

commit v5 on v4

--- a/solution.py
+++ b/solution.py
@@ -66,6 +66,14 @@
         (pad_two, place_two, top_two, side_two, rows_two, cols_two),
     )
 
+    barrier = pltpu.get_barrier_semaphore()
+    sides = ((has_up, up), (has_down, down), (has_left, left), (has_right, right))
+    for there, device in sides:
+
+        @pl.when(there)
+        def _():
+            pl.semaphore_signal(barrier, inc=1, device_id=device, device_id_type=MESH)
+
     local = [
         pltpu.make_async_copy(tables_hbm, tables, local_sem.at[0]),
         pltpu.make_async_copy(phase_hbm, phase, local_sem.at[1]),
@@ -86,16 +94,8 @@
         for which, pad in enumerate((pad_one, pad_two))
     ]
     local += inner[0] + inner[1]
-    for copy in local:
+    for copy in local[:3]:
         copy.start()
-
-    barrier = pltpu.get_barrier_semaphore()
-    sides = ((has_up, up), (has_down, down), (has_left, left), (has_right, right))
-    for there, device in sides:
-
-        @pl.when(there)
-        def _():
-            pl.semaphore_signal(barrier, inc=1, device_id=device, device_id_type=MESH)
 
     pl.semaphore_wait(barrier, sum(there.astype(jnp.int32) for there, _ in sides))
 
@@ -185,6 +185,8 @@
 
     (rows_a, cols_a, corners_a), (rows_b, cols_b, corners_b) = halos
     start(rows_a[:4] + rows_b[:4] + cols_a)
+    for copy in local[3:]:
+        copy.start()
 
     for pad in (pad_one, pad_two):
 
@@ -353,7 +355,7 @@
             im = jnp.concatenate([total[rows, half:], difference[rows, half:]], 1)
             after(c, rows, re, im)
 
-    def frames(steps_of, then=None):
+    def frames(steps_of, then=None, at_once=False):
         def group(number, nothing):
             running = [steps_of(which, number * GROUP + which) for which in range(GROUP)]
             while running:
@@ -362,7 +364,12 @@
                 then(number)
             return nothing
 
-        lax.fori_loop(0, cap // GROUP, group, 0)
+        if at_once:
+            running = [steps_of(which, which) for which in range(cap)]
+            while running:
+                running = [steps for steps in running if next(steps, steps_end) is not steps_end]
+        else:
+            lax.fori_loop(0, cap // GROUP, group, 0)
 
     wait_recv(rows_b[:4])
     start(corners_b + rows_b[4:])
@@ -408,7 +415,7 @@
 
         return there_and_back(which, before, between, after)
 
-    frames(leave)
+    frames(leave, at_once=True)
 
     blocks = ext // half
     last = blocks - 1
@@ -463,10 +470,10 @@
 
     def send_sums(which):
         rows, cols, corners = folds[which]
+        gather_top(which, 2, 1)
+        start(rows[4:])
         gather_top(which, 0, last)
         start(corners)
-        gather_top(which, 2, 1)
-        start(rows[4:])
         gather_top(which, 1, last - 2)
         gather_sides(which)
         start(cols)
@@ -565,8 +572,8 @@
         pltpu.VMEM((frame, frame), F32),
         pltpu.VMEM((4, 3 * frame, frame), BF16),
         pltpu.VMEM((4, frame, 3 * frame), BF16),
-        pltpu.VMEM((GROUP, 2, frame, 2 * frame), BF16),
-        pltpu.VMEM((GROUP, 2, 2 * frame, frame), BF16),
+        pltpu.VMEM((cap, 2, frame, 2 * frame), BF16),
+        pltpu.VMEM((cap, 2, 2 * frame, frame), BF16),
         pltpu.SMEM((2, cap), jnp.int32),
         pltpu.SMEM((1,), jnp.int32),
         pltpu.SemaphoreType.DMA((4 * COPIES,)),

time: 62.5 us -> 62 us (level)
  no operation moved by 1% of the time
where the time goes in v5:
time: 62 us; the launch traced here: 61.8 us
  Pallas kernels  59.1 us (95%)
  local copies, waits for them, and re-layouts  2.02 us (3%)
  between operations  0.66 us (1%)
    pallas_call x1, Pallas kernels, shards(): pl.pallas_call(functools.partial(kernel, n_gx, n_gy), out_shape=pltpu.VME...  59.1 us
    unnamed x1, local copies, waits for them, and re-layouts  2.02 us

profile of v5, /device:TPU:57, one launch (start us, length us, event | category | flops | bytes accessed | tf_op | source)
XLA Modules:
  0.0 61.8 jit_solution(11998498020270023844)
XLA Ops:
  0.7 59.1 %ptychography.1 = f32[4,512,512]{2,1,0:T(8,128)S(1)} custom-call(s32[2,4]{1,0:T(2,128)} %bitcast.1, s32[1]{0:T(128)S(6)} %copy.10.counts_hbm, f32[4,512,512]{2,1,0:T(8,128)} %objects.1, f32[2,256,256]{2,1,0:T(8,128)} %probe_hbm.1, f32[256,256]{1,0:T(8,128)} %phase_hbm.1, f32[4,256,256]{2,1,0:T(8,128)} %intensity_hbm.1, f32[6,128,128]{2,1,0:T(8,128)} %constant.2.clone.tables_hbm), custom_call_target="tpu_custom_call" | custom-call | tf_op jit(solution)/shard_map/ptychography/pallas_call | solution.py:584
  59.8 2.0 %copy.9 = f32[4,512,512]{2,1,0:T(8,128)} copy(f32[4,512,512]{2,1,0:T(8,128)S(1)} %ptychography.1) | data formatting | bytes 8388608

commit v6 on v5

--- a/solution.py
+++ b/solution.py
@@ -435,16 +435,16 @@
     def block_at(number):
         return pl.ds(pl.multiple_of(number * half, half), half)
 
-    def gather_top(which, first_col, step_col):
+    def gather_top(which, edge, first_col, step_col):
         top = slices[which][2]
 
         def step(number, nothing):
-            edge, col_block = number // 2, first_col + number % 2 * step_col
+            col_block = first_col + number * step_col
             for comp in range(2):
                 top[comp, edge, :, block_at(col_block)] = gathered(which, comp, edge * last, col_block)
             return nothing
 
-        lax.fori_loop(0, 4, step, 0)
+        lax.fori_loop(0, 2, step, 0)
 
     def gather_sides(which):
         side = slices[which][3]
@@ -470,11 +470,14 @@
 
     def send_sums(which):
         rows, cols, corners = folds[which]
-        gather_top(which, 2, 1)
-        start(rows[4:])
-        gather_top(which, 0, last)
-        start(corners)
-        gather_top(which, 1, last - 2)
+        for edge in range(2):
+            gather_top(which, edge, 2, 1)
+            start(rows[4 + edge : 5 + edge])
+        for edge in range(2):
+            gather_top(which, edge, 0, last)
+            start(corners[2 * edge : 2 * edge + 2])
+        for edge in range(2):
+            gather_top(which, edge, 1, last - 2)
         gather_sides(which)
         start(cols)
         gather_inner(which)
@@ -540,11 +543,11 @@
     send_sums(0)
     pass_corners(0)
     finish(1)
+    wait_send(rows_a[4:] + cols_a + corners_a + rows_b + cols_b + corners_b)
+    for copies in (*folds[1], folds[0][0][4:], *folds[0][1:]):
+        wait_send(copies)
     finish(0)
-    wait_send(rows_a[4:] + cols_a + corners_a)
-    for exchange in [halos[1], *folds]:
-        for copies in exchange:
-            wait_send(copies)
+    wait_send(folds[0][0][:4])
 
 
 def shards(n_gx, n_gy, objects, probe_wave, prop_phase, intensity, offsets, counts):

time: 62 us -> 61.8 us (level)
  no operation moved by 1% of the time
where the time goes in v6:
time: 61.8 us; the launch traced here: 61.7 us
  Pallas kernels  59 us (95%)
  local copies, waits for them, and re-layouts  2.02 us (3%)
  between operations  0.66 us (1%)
    pallas_call x1, Pallas kernels, shards(): pl.pallas_call(functools.partial(kernel, n_gx, n_gy), out_shape=pltpu.VME...  59 us
    unnamed x1, local copies, waits for them, and re-layouts  2.02 us

profile of v6, /device:TPU:57, one launch (start us, length us, event | category | flops | bytes accessed | tf_op | source)
XLA Modules:
  0.0 61.7 jit_solution(10690569914404479570)
XLA Ops:
  0.7 59.0 %ptychography.1 = f32[4,512,512]{2,1,0:T(8,128)S(1)} custom-call(s32[2,4]{1,0:T(2,128)} %bitcast.1, s32[1]{0:T(128)S(6)} %copy.10.counts_hbm, f32[4,512,512]{2,1,0:T(8,128)} %objects.1, f32[2,256,256]{2,1,0:T(8,128)} %probe_hbm.1, f32[256,256]{1,0:T(8,128)} %phase_hbm.1, f32[4,256,256]{2,1,0:T(8,128)} %intensity_hbm.1, f32[6,128,128]{2,1,0:T(8,128)} %constant.2.clone.tables_hbm), custom_call_target="tpu_custom_call" | custom-call | tf_op jit(solution)/shard_map/ptychography/pallas_call | solution.py:587
  59.7 2.0 %copy.9 = f32[4,512,512]{2,1,0:T(8,128)} copy(f32[4,512,512]{2,1,0:T(8,128)S(1)} %ptychography.1) | data formatting | bytes 8388608

commit v7 on v6

--- a/solution.py
+++ b/solution.py
@@ -390,7 +390,7 @@
 
         return there_and_back(which, before, between, after)
 
-    frames(enter)
+    frames(enter, at_once=True)
 
     wait_recv(rows_b[4:] + cols_b + corners_b)
     for copy in inner[1]:

time: 61.8 us -> 61.8 us (level)
  no operation moved by 1% of the time
where the time goes in v7:
time: 61.8 us; the launch traced here: 61.7 us
  Pallas kernels  59 us (95%)
  local copies, waits for them, and re-layouts  2.02 us (3%)
  between operations  0.66 us (1%)
    pallas_call x1, Pallas kernels, shards(): pl.pallas_call(functools.partial(kernel, n_gx, n_gy), out_shape=pltpu.VME...  59 us
    unnamed x1, local copies, waits for them, and re-layouts  2.02 us

profile of v7, /device:TPU:57, one launch (start us, length us, event | category | flops | bytes accessed | tf_op | source)
XLA Modules:
  0.0 61.7 jit_solution(1577188108648026549)
XLA Ops:
  0.7 59.0 %ptychography.1 = f32[4,512,512]{2,1,0:T(8,128)S(1)} custom-call(s32[2,4]{1,0:T(2,128)} %bitcast.1, s32[1]{0:T(128)S(6)} %copy.10.counts_hbm, f32[4,512,512]{2,1,0:T(8,128)} %objects.1, f32[2,256,256]{2,1,0:T(8,128)} %probe_hbm.1, f32[256,256]{1,0:T(8,128)} %phase_hbm.1, f32[4,256,256]{2,1,0:T(8,128)} %intensity_hbm.1, f32[6,128,128]{2,1,0:T(8,128)} %constant.2.clone.tables_hbm), custom_call_target="tpu_custom_call" | custom-call | tf_op jit(solution)/shard_map/ptychography/pallas_call | solution.py:587
  59.7 2.0 %copy.9 = f32[4,512,512]{2,1,0:T(8,128)} copy(f32[4,512,512]{2,1,0:T(8,128)S(1)} %ptychography.1) | data formatting | bytes 8388608
